TPU v7x, 32 devices: a whole 2x2x4 slice. The times are simulated.
32 devices in a mesh: ent: 8 (over z, x), qry: 4 (over y, core).
Axes of the slice: x: 2, y: 2, z: 4, core: 2. Of those that a mesh axis runs over, the one named last changes fastest.
Arguments:
- ent_feat: bfloat16 [64, 8192], P(None, 'ent'), may hold values from -6 to 6
- query_head: int32 [16], replicated, may hold values from 0 to 8191
- query_rel: int32 [16], replicated, may hold values from 0 to 821
- query_table: bfloat16 [822, 64], replicated, may hold values from -5 to 5
- rel_table: bfloat16 [3, 822, 64], replicated, may hold values from -5 to 5
- layer_weight: bfloat16 [3, 64, 64], replicated, may hold values from -0.75 to 0.75
- layer_bias: float32 [3, 64], replicated, may hold values from -5 to 5
- norm_gain: float32 [3, 64], replicated, may hold values from 0.5 to 1.5
- norm_shift: float32 [3, 64], replicated, may hold values from -3 to 3
- reg_blocks: int32 [640, 2], P('ent'), may hold values from 0 to 63, as said below
- reg_rel: int32 [640], P('ent'), may hold values from 0 to 821
- reg_mask: int32 [640, 128, 128], P('ent'), may hold values 0 or 1
- hin_blocks: int32 [192, 2], P('ent'), may hold values from 0 to 63, as said below
- hin_rel: int32 [192], P('ent'), may hold values from 0 to 821
- hin_mask: int32 [192, 128, 128], P('ent'), may hold values 0 or 1
- hout_blocks: int32 [192, 2], P('ent'), may hold values from 0 to 63, as said below
- hout_rel: int32 [192], P('ent'), may hold values from 0 to 821
- hout_mask: int32 [192, 128, 128], P('ent'), may hold values 0 or 1
- read_weight: bfloat16 [128, 64], replicated, may hold values from -0.5 to 0.5
- read_bias: float32 [64], replicated, may hold values from -5 to 5
- read_out: float32 [64], replicated, may hold values from -0.75 to 0.75
Outputs:
- scores: float32 [16, 8192], P(None, ('ent', 'qry'))
- hub_scores: float32 [16, 128], P('qry', 'ent')
Inputs may be any that keep to these rules, and one draw needn't show every extreme that they name: `reg_blocks`: rows are grouped by 80 per index of ent. Column 0 is a block of that index's own 8 blocks; column 1 is a block of the same index's or an adjacent index's entities. `hin_blocks`: rows are grouped by 24 per index of ent. Column 0 is a hub block, below 1; column 1 is a block of that index's own entities. `hout_blocks`: rows are grouped by 24 per index of ent. Column 0 is a block of that index's own entities; column 1 is a hub block, below 1.
All inputs are finite; a program needn't handle non-finite values. No bound on the sum of `reg_mask` or of `hin_mask` or of `hout_mask` on one device may be relied on, other than what follows from the above.
Results may differ from a plain program's by a relative error of at most 0.0075.
Values may be sent and summed in bfloat16 or wider, within the bound.
No kernel may reach another device: no remote copies, remote signals or barrier semaphores. Data moves between devices by JAX's collectives and lax.ppermute only.
A program may use at most 128 MiB of HBM per device.

v0:
```python
import jax
import jax.numpy as jnp
from jax import lax
from jax.sharding import PartitionSpec as P

LAYERS = 3
HUB_DEV = 16


def padded(cells, sides, width):
    for axis, dim in sides:
        count = lax.axis_size(axis)
        ends = count - 1
        head = lax.slice_in_dim(cells, 0, width, axis=dim)
        tail = lax.slice_in_dim(cells, cells.shape[dim] - width, cells.shape[dim], axis=dim)
        cells = jnp.concatenate(
            [
                lax.ppermute(tail, axis, [(i, (i + 1) % count) for i in range(ends)]),
                cells,
                lax.ppermute(head, axis, [((i + 1) % count, i) for i in range(ends)]),
            ],
            axis=dim,
        )
    return cells


def normalize(values, along_axis, gain_rows, shift_rows):
    average = jnp.mean(values, axis=along_axis, keepdims=True)
    centered = values - average
    variance = jnp.mean(centered * centered, axis=along_axis, keepdims=True)
    return centered * lax.rsqrt(variance + 1e-05) * gain_rows + shift_rows


def update_hubs(hub_sum, hub_old, weight, bias_row, gain_row, shift_row, q_local, model_width):
    count = hub_sum.shape[0]
    inputs_now = hub_sum.astype(jnp.bfloat16).reshape(count, q_local, model_width)
    linear = (
        jnp.einsum("hqd,de->hqe", inputs_now, weight, preferred_element_type=jnp.float32)
        + bias_row[None, None, :]
    )
    normed = normalize(linear, 2, gain_row[None, None, :], shift_row[None, None, :])
    updated = jax.nn.relu(normed) + hub_old.astype(jnp.float32).reshape(count, q_local, model_width)
    return updated.astype(jnp.bfloat16).reshape(count, q_local * model_width)


def body(
    ent_feat,
    query_head,
    query_rel,
    query_table,
    rel_table,
    layer_weight,
    layer_bias,
    norm_gain,
    norm_shift,
    reg_blocks,
    reg_rel,
    reg_mask,
    hin_blocks,
    hin_rel,
    hin_mask,
    hout_blocks,
    hout_rel,
    hout_mask,
    read_weight,
    read_bias,
    read_out,
):
    ent_devices = lax.axis_size("ent")
    queries = query_head.shape[0]
    q_local = queries // lax.axis_size("qry")
    model_width = ent_feat.shape[0]
    ent_local = ent_feat.shape[1]
    block_size = reg_mask.shape[1]
    blocks_local = ent_local // block_size
    hub_total = HUB_DEV * ent_devices
    hub_block_count = hub_total // block_size
    state_rows = q_local * model_width
    first_block = lax.axis_index("ent") * blocks_local
    first_entity = lax.axis_index("ent") * ent_local
    query_first = lax.axis_index("qry") * q_local
    highest = lax.Precision.HIGHEST
    rel_iota = jnp.arange(query_table.shape[0], dtype=jnp.int32)
    query_onehot = (query_rel[:, None] == rel_iota[None, :]).astype(jnp.bfloat16)
    query_all = jnp.dot(query_onehot, query_table, preferred_element_type=jnp.float32)
    query_local = lax.dynamic_slice_in_dim(query_all, query_first, q_local, 0)
    heads_local = lax.dynamic_slice_in_dim(query_head, query_first, q_local, 0)
    positions = first_entity + jnp.arange(ent_local, dtype=jnp.int32)
    head_hits = (heads_local[:, None] == positions[None, :]).astype(jnp.float32)
    boundary = query_local[:, :, None] * head_hits[:, None, :]
    states = (ent_feat.astype(jnp.float32)[None] + boundary).astype(jnp.bfloat16)
    reg_masks = reg_mask.astype(jnp.bfloat16)
    hin_masks = hin_mask.astype(jnp.bfloat16)
    hout_masks = hout_mask.astype(jnp.bfloat16)
    local_iota = jnp.arange(blocks_local, dtype=jnp.int32)[None, :]
    reg_onehot = (reg_blocks[:, 0][:, None] - first_block == local_iota).astype(jnp.float32)
    reg_sources = reg_blocks[:, 1] - first_block + blocks_local
    hout_onehot = (hout_blocks[:, 0][:, None] - first_block == local_iota).astype(jnp.float32)
    hout_sources = hout_blocks[:, 1]
    hin_onehot = (
        hin_blocks[:, 0][:, None] == jnp.arange(hub_block_count, dtype=jnp.int32)[None, :]
    ).astype(jnp.float32)
    hin_sources = hin_blocks[:, 1] - first_block

    def tile_coefficients(rel_ids, rel_layer):
        rel_onehot = (rel_ids[:, None] == rel_iota[None, :]).astype(jnp.bfloat16)
        rel_rows = jnp.dot(rel_onehot, rel_layer, preferred_element_type=jnp.float32)
        return (query_local[:, :, None] * rel_rows.T[None, :, :]).reshape(state_rows, -1)

    hub_own = jnp.zeros((HUB_DEV, state_rows), jnp.bfloat16)
    for layer_at in range(LAYERS):
        weight = layer_weight[layer_at]
        rel_layer = rel_table[layer_at]
        flat_states = states.reshape(state_rows, ent_local)
        window = padded(flat_states, (("ent", 1),), ent_local)
        window_blocks = window.reshape(state_rows, 3 * blocks_local, block_size)
        gathered = jnp.take(window_blocks, reg_sources, axis=1)
        product = jnp.einsum(
            "ctj,tjk->ctk", gathered, reg_masks, preferred_element_type=jnp.float32
        )
        product = product * tile_coefficients(reg_rel, rel_layer)[:, :, None]
        totals = jnp.einsum("ctk,tb->cbk", product, reg_onehot, precision=highest)
        if layer_at > 0:
            hub_full = lax.all_gather(hub_own, "ent", axis=0, tiled=True)
        else:
            hub_full = jnp.zeros((hub_total, state_rows), jnp.bfloat16)
        hub_view = hub_full.reshape(hub_block_count, block_size, state_rows)
        hub_sources = jnp.take(hub_view, hout_sources, axis=0)
        product = jnp.einsum(
            "tjc,tjk->ctk", hub_sources, hout_masks, preferred_element_type=jnp.float32
        )
        product = product * tile_coefficients(hout_rel, rel_layer)[:, :, None]
        totals = totals + jnp.einsum("ctk,tb->cbk", product, hout_onehot, precision=highest)
        own_blocks = flat_states.reshape(state_rows, blocks_local, block_size)
        hin_gathered = jnp.take(own_blocks, hin_sources, axis=1)
        hin_product = jnp.einsum(
            "ctj,tjk->tkc", hin_gathered, hin_masks, preferred_element_type=jnp.float32
        )
        hin_product = hin_product * tile_coefficients(hin_rel, rel_layer).T[:, None, :]
        partial_value = jnp.einsum(
            "tkc,th->hkc", hin_product, hin_onehot, precision=highest
        ).reshape(hub_total, state_rows)
        inputs_now = (totals.reshape(q_local, model_width, ent_local) + boundary).astype(
            jnp.bfloat16
        )
        linear = (
            jnp.einsum("qdv,de->qev", inputs_now, weight, preferred_element_type=jnp.float32)
            + layer_bias[layer_at][None, :, None]
        )
        normed = normalize(
            linear, 1, norm_gain[layer_at][None, :, None], norm_shift[layer_at][None, :, None]
        )
        states = (jax.nn.relu(normed) + states.astype(jnp.float32)).astype(jnp.bfloat16)
        hub_sum = lax.psum_scatter(partial_value, "ent", scatter_dimension=0, tiled=True)
        hub_own = update_hubs(
            hub_sum,
            hub_own,
            weight,
            layer_bias[layer_at],
            norm_gain[layer_at],
            norm_shift[layer_at],
            q_local,
            model_width,
        )
    read_states = read_weight[:model_width]
    query_part_all = (
        jnp.dot(
            query_all.astype(jnp.bfloat16),
            read_weight[model_width:],
            preferred_element_type=jnp.float32,
        )
        + read_bias[None, :]
    )
    query_part_local = lax.dynamic_slice_in_dim(query_part_all, query_first, q_local, 0)
    moved_states = lax.all_to_all(states, "qry", split_axis=2, concat_axis=0, tiled=True)
    features = jax.nn.relu(
        jnp.einsum("qdv,de->qev", moved_states, read_states, preferred_element_type=jnp.float32)
        + query_part_all[:, :, None]
    )
    scores = jnp.einsum("qev,e->qv", features, read_out, precision=highest)
    hub_view_own = hub_own.reshape(HUB_DEV, q_local, model_width)
    hub_features = jax.nn.relu(
        jnp.einsum("hqd,de->hqe", hub_view_own, read_states, preferred_element_type=jnp.float32)
        + query_part_local[None]
    )
    hub_scores = jnp.einsum("hqe,e->qh", hub_features, read_out, precision=highest)
    return (scores, hub_scores)


def solution(mesh):
    return jax.shard_map(
        body,
        mesh=mesh,
        in_specs=(
            P(None, "ent"),
            P(),
            P(),
            P(),
            P(),
            P(),
            P(),
            P(),
            P(),
            P("ent", None),
            P("ent"),
            P("ent", None, None),
            P("ent", None),
            P("ent"),
            P("ent", None, None),
            P("ent", None),
            P("ent"),
            P("ent", None, None),
            P(),
            P(),
            P(),
        ),
        out_specs=(P(None, ("ent", "qry")), P("qry", "ent")),
        check_vma=False,
    )
```

profile of v0, /device:TPU:0, one launch (start us, length us, event | category | flops | bytes accessed | tf_op | source)
XLA Modules:
  0.0 461.3 jit_solution(1653198230750983543)
XLA Ops:
  13.4 6.3 %collective-permute-start = (bf16[256,1024]{1,0:T(8,128)(2,1)}, bf16[256,1024]{1,0:T(8,128)(2,1)}, u32[]{:S(2)}, u32[]{:S(2)}) collective-permute-start(bf16[256,1024]{1,0:T(8,128)(2,1)} %fusion.90), channel_id=1, source_target_pairs={{0,4},{4,8},{8,12},{12,16},{16,20},{20,24},{24,28},{1,5},{5,9},{9,... | collective-permute-start | bytes 1572872 | tf_op jit(solution)/shard_map/ppermute | solution.py:18
  37.9 4.0 multiply_bitcast_fusion.2
  56.1 3.9 fusion.28
  64.0 48.3 %reduce-scatter.4.cloned.1.call-done = f32[16,256]{1,0:T(8,128)} async-done(((f32[128,256]{1,0:T(8,128)}), f32[16,256]{1,0:T(8,128)}) %reduce-scatter.4.cloned.1.call-update) | async-done | bytes 16400 | tf_op jit(solution)/shard_map/reduce_scatter | solution.py:154
  117.5 5.9 %gather_fusion = bf16[80,256,128]{2,1,0:T(8,128)(2,1)} fusion(bf16[256,24,128]{2,0,1:T(8,128)(2,1)S(1)} %copy.179, s32[1024]{0:T(1024)} %pad_clamp_fusion.1), kind=kCustom, calls=%fused_computation.clone | custom fusion | bytes 10486080 | tf_op jit(solution)/shard_map/jit(_take)/gather | solution.py:117
  123.5 6.6 %bitcast_multiply_fusion.2 = f32[256,80,128]{2,0,1:T(8,128)S(1)} fusion(f32[256,80]{0,1:T(8,128)S(1)} %copy-done.19, bf16[80,256,128]{2,1,0:T(8,128)(2,1)} %gather_fusion, pred[80]{0:T(512)(128)(4,1)S(1)} %copy-done.37, s32[80,128,128]{2,1,0:T(8,128)} %param.38), kind=kOutput, calls=%fused_computation.8 | convolution fusion | flops 677642240 | bytes 21053520 | tf_op jit(solution)/shard_map/ctj,tjk->ctk/dot_general | solution.py:118
  130.1 9.4 %fusion.78 = bf16[256,8,128]{2,1,0:T(8,128)(2,1)S(1)} fusion(f32[256,8,128]{2,1,0:T(8,128)S(1)} %get-tuple-element.12, f32[8,256,128]{2,0,1:T(8,128)S(1)} %copy-done.15, f32[256,80,128]{2,0,1:T(8,128)S(1)} %bitcast_multiply_fusion.2, s32[80]{0:T(128)S(1)} %copy-done.43), kind=kOutput, calls=%fused_computation.76 | convolution fusion | flops 252445312 | bytes 13107520 | tf_op jit(solution)/shard_map/ctk,tb->cbk/dot_general | solution.py:122
  145.9 4.4 multiply_bitcast_fusion.1
  162.6 5.4 %collective-permute-start.2 = (bf16[256,1024]{0,1:T(8,128)(2,1)}, bf16[256,1024]{0,1:T(8,128)(2,1)}, u32[]{:S(2)}, u32[]{:S(2)}) collective-permute-start(bf16[256,1024]{0,1:T(8,128)(2,1)} %copy.184), channel_id=1, source_target_pairs={{0,4},{4,8},{8,12},{12,16},{16,20},{20,24},{24,28},{1,5},{5,9},{9,... | collective-permute-start | bytes 1572872 | tf_op jit(solution)/shard_map/ppermute | solution.py:18
  168.0 52.6 %reduce-scatter.6.cloned.1.call-done = f32[16,256]{1,0:T(8,128)} async-done(((f32[128,256]{1,0:T(8,128)}), f32[16,256]{1,0:T(8,128)}) %reduce-scatter.6.cloned.1.call-update) | async-done | bytes 16400 | tf_op jit(solution)/shard_map/reduce_scatter | solution.py:154
  226.0 32.4 %all_gather.6 = bf16[128,256]{1,0:T(8,128)(2,1)} all-gather(bf16[16,256]{1,0:T(8,128)(2,1)S(1)} %reshape.378), channel_id=1, replica_groups=mesh['ent'=8,'qry'=4] {'ent'}, dimensions={0}, use_global_device_ids=true | all-gather | bytes 73728 | tf_op jit(solution)/shard_map/all_gather | solution.py:124
  260.7 32.4 %all_gather.7 = bf16[128,256]{1,0:T(8,128)(2,1)} all-gather(bf16[16,256]{1,0:T(8,128)(2,1)S(1)} %reshape.382), channel_id=1, replica_groups=mesh['ent'=8,'qry'=4] {'ent'}, dimensions={0}, use_global_device_ids=true | all-gather | bytes 73728 | tf_op jit(solution)/shard_map/all_gather | solution.py:124
  296.5 3.8 fusion.26
  308.3 5.9 %gather_fusion.1 = bf16[80,256,128]{2,1,0:T(8,128)(2,1)} fusion(bf16[256,24,128]{2,0,1:T(8,128)(2,1)S(1)} %pad_maximum_fusion.1, s32[1024]{0:T(1024)} %pad_clamp_fusion.1), kind=kCustom, calls=%fused_computation.2.clone | custom fusion | bytes 10486080 | tf_op jit(solution)/shard_map/jit(_take)/gather | solution.py:117
  314.2 6.5 %bitcast_multiply_fusion.1 = f32[256,80,128]{2,0,1:T(8,128)S(1)} fusion(f32[256,80]{0,1:T(8,128)S(1)} %copy-done.18, bf16[80,256,128]{2,1,0:T(8,128)(2,1)} %gather_fusion.1, pred[80]{0:T(512)(128)(4,1)S(1)} %copy-done.38, s32[80,128,128]{2,1,0:T(8,128)} %param.38), kind=kOutput, calls=%fused_computation.7 | convolution fusion | flops 677642240 | bytes 21053520 | tf_op jit(solution)/shard_map/ctj,tjk->ctk/dot_general | solution.py:118
  320.8 9.4 %fusion.81 = bf16[256,8,128]{2,1,0:T(8,128)(2,1)S(1)} fusion(f32[256,8,128]{2,1,0:T(8,128)S(1)} %get-tuple-element.12, f32[8,256,128]{2,0,1:T(8,128)S(1)} %copy-done.17, f32[256,80,128]{2,0,1:T(8,128)S(1)} %bitcast_multiply_fusion.1, s32[80]{0:T(128)S(1)} %copy-done.44), kind=kOutput, calls=%fused_computation.77 | convolution fusion | flops 252445312 | bytes 13107520 | tf_op jit(solution)/shard_map/ctk,tb->cbk/dot_general | solution.py:122
  336.2 4.2 multiply_bitcast_fusion
  347.8 5.7 %fusion.24 = f32[8,256,128]{2,0,1:T(8,128)} fusion(f32[256,24,128]{2,0,1:T(8,128)} %bitcast_multiply_fusion.3, s32[24]{0:T(128)S(1)} %copy-done.48), kind=kOutput, calls=%fused_computation.30 | convolution fusion | flops 75497664 | bytes 4194400 | tf_op jit(solution)/shard_map/ctk,tb->cbk/dot_general | solution.py:133
  355.0 4.6 collective-permute-start.4
  359.6 49.5 %reduce-scatter.8.cloned.1.call-done = f32[16,256]{1,0:T(8,128)} async-done(((f32[128,256]{1,0:T(8,128)}), f32[16,256]{1,0:T(8,128)}) %reduce-scatter.8.cloned.1.call-update) | async-done | bytes 16400 | tf_op jit(solution)/shard_map/reduce_scatter | solution.py:154
  413.7 5.8 %gather_fusion.3 = bf16[80,256,128]{2,1,0:T(8,128)(2,1)} fusion(bf16[256,24,128]{2,0,1:T(8,128)(2,1)S(1)} %pad_maximum_fusion.2, s32[1024]{0:T(1024)} %pad_clamp_fusion.1), kind=kCustom, calls=%fused_computation.3.clone | custom fusion | bytes 10486080 | tf_op jit(solution)/shard_map/jit(_take)/gather | solution.py:117
  419.5 6.6 %bitcast_multiply_fusion = f32[256,80,128]{2,0,1:T(8,128)S(1)} fusion(f32[256,80]{0,1:T(8,128)S(1)} %copy.203, bf16[80,256,128]{2,1,0:T(8,128)(2,1)} %gather_fusion.3, pred[80]{0:T(512)(128)(4,1)S(1)} %copy-done.38, s32[80,128,128]{2,1,0:T(8,128)} %param.38), kind=kOutput, calls=%fused_computation.6 | convolution fusion | flops 677642240 | bytes 21053520 | tf_op jit(solution)/shard_map/ctj,tjk->ctk/dot_general | solution.py:118
  426.1 9.4 %fusion.84 = bf16[256,8,128]{2,1,0:T(8,128)(2,1)S(1)} fusion(f32[256,8,128]{2,1,0:T(8,128)S(1)} %get-tuple-element.12, f32[8,256,128]{2,0,1:T(8,128)S(1)} %copy-done.16, f32[256,80,128]{2,0,1:T(8,128)S(1)} %bitcast_multiply_fusion, s32[80]{0:T(128)S(1)} %copy-done.45), kind=kOutput, calls=%fused_computation.78 | convolution fusion | flops 252445312 | bytes 13107520 | tf_op jit(solution)/shard_map/ctk,tb->cbk/dot_general | solution.py:122
  443.9 7.6 %all-to-all-done = bf16[4,2,32768]{2,1,0:T(2,128)(2,1)S(1)} async-done(((bf16[4,2,32768]{2,1,0:T(2,128)(2,1)}), bf16[4,2,32768]{2,1,0:T(2,128)(2,1)S(1)}, u32[]{:S(2)}, u32[]{:S(2)}) %all-to-all-start) | async-done | bytes 524320 | tf_op jit(solution)/shard_map/all_to_all | solution.py:175
  (278 shorter events, 115.4 us)
Async XLA Ops:
  7.2 105.1 %reduce-scatter.4.cloned.1.call-start = ((), (), s32[]{:S(2)}) async-start(), calls=%async_computation.4 | async-start | bytes 147456 | tf_op jit(solution)/shard_map/reduce_scatter | solution.py:154
  12.1 102.5 %collective-permute-start.1 = (bf16[256,1024]{1,0:T(8,128)(2,1)}, bf16[256,1024]{1,0:T(8,128)(2,1)}, u32[]{:S(2)}, u32[]{:S(2)}) collective-permute-start(bf16[256,1024]{1,0:T(8,128)(2,1)} %fusion.90), channel_id=1, source_target_pairs={{4,0},{8,4},{12,8},{16,12},{20,16},{24,20},{28,24},{5,1},{9,5},{13... | collective-permute-start | bytes 1572872 | tf_op jit(solution)/shard_map/ppermute | solution.py:20
  13.4 102.4 %collective-permute-start = (bf16[256,1024]{1,0:T(8,128)(2,1)}, bf16[256,1024]{1,0:T(8,128)(2,1)}, u32[]{:S(2)}, u32[]{:S(2)}) collective-permute-start(bf16[256,1024]{1,0:T(8,128)(2,1)} %fusion.90), channel_id=1, source_target_pairs={{0,4},{4,8},{8,12},{12,16},{16,20},{20,24},{24,28},{1,5},{5,9},{9,... | collective-permute-start | bytes 1572872 | tf_op jit(solution)/shard_map/ppermute | solution.py:18
  45.5 8.8 %copy-start.61 = (s32[80,2]{0,1:T(2,128)S(1)}, s32[80,2]{0,1:T(2,128)}, u32[]{:S(2)}) copy-start(s32[80,2]{0,1:T(2,128)} %param.36) | copy-start | bytes 1924
  45.5 9.2 %copy-start.4 = (s32[24,128,128]{2,1,0:T(8,128)S(1)}, s32[24,128,128]{2,1,0:T(8,128)}, u32[]{:S(2)}) copy-start(s32[24,128,128]{2,1,0:T(8,128)} %param.44) | copy-start | bytes 4718596
  49.4 171.2 %reduce-scatter.6.cloned.1.call-start = ((), (), s32[]{:S(2)}) async-start(), calls=%async_computation.5 | async-start | bytes 147456 | tf_op jit(solution)/shard_map/reduce_scatter | solution.py:154
  50.2 9.7 %copy-start.46 = (s32[24]{0:T(128)}, s32[24]{0:T(128)S(1)}, u32[]{:S(2)}) copy-start(s32[24]{0:T(128)S(1)} %subtract_bitcast_fusion) | copy-start | bytes 292
  54.3 58.8 %copy-start.50 = (f32[64]{0:T(128)}, f32[64]{0:T(128)S(1)}, u32[]{:S(2)}) copy-start(f32[64]{0:T(128)S(1)} %get-tuple-element.22) | copy-start | bytes 772
  56.0 60.8 %copy-start.14 = (bf16[256,8,128]{2,1,0:T(8,128)(2,1)S(1)}, bf16[256,8,128]{2,1,0:T(8,128)(2,1)}, u32[]{:S(2)}) copy-start(bf16[256,8,128]{2,1,0:T(8,128)(2,1)} %copy-done.13) | copy-start | bytes 1572868
  60.7 51.6 %copy-start.29 = (f32[16,64]{1,0:T(8,128)}, f32[16,64]{1,0:T(8,128)S(1)}, u32[]{:S(2)}) copy-start(f32[16,64]{1,0:T(8,128)S(1)} %convolution_add_fusion.8) | copy-start | bytes 12292
  130.1 9.6 %copy-start.51 = (f32[64]{0:T(128)S(1)}, f32[64]{0:T(128)}, u32[]{:S(2)}) copy-start(f32[64]{0:T(128)} %copy-done.50) | copy-start | bytes 772
  153.9 140.8 %copy-start.5 = (s32[24,128,128]{2,1,0:T(8,128)S(1)}, s32[24,128,128]{2,1,0:T(8,128)}, u32[]{:S(2)}) copy-start(s32[24,128,128]{2,1,0:T(8,128)} %param.44) | copy-start | bytes 4718596
  157.8 251.2 %reduce-scatter.8.cloned.1.call-start = ((), (), s32[]{:S(2)}) async-start(), calls=%async_computation.6 | async-start | bytes 147456 | tf_op jit(solution)/shard_map/reduce_scatter | solution.py:154
  161.3 141.4 %collective-permute-start.3 = (bf16[256,1024]{0,1:T(8,128)(2,1)}, bf16[256,1024]{0,1:T(8,128)(2,1)}, u32[]{:S(2)}, u32[]{:S(2)}) collective-permute-start(bf16[256,1024]{0,1:T(8,128)(2,1)} %copy.184), channel_id=1, source_target_pairs={{4,0},{8,4},{12,8},{16,12},{20,16},{24,20},{28,24},{5,1},{9,5},{13... | collective-permute-start | bytes 1572872 | tf_op jit(solution)/shard_map/ppermute | solution.py:20
  162.6 142.2 %collective-permute-start.2 = (bf16[256,1024]{0,1:T(8,128)(2,1)}, bf16[256,1024]{0,1:T(8,128)(2,1)}, u32[]{:S(2)}, u32[]{:S(2)}) collective-permute-start(bf16[256,1024]{0,1:T(8,128)(2,1)} %copy.184), channel_id=1, source_target_pairs={{0,4},{4,8},{8,12},{12,16},{16,20},{20,24},{24,28},{1,5},{5,9},{9,... | collective-permute-start | bytes 1572872 | tf_op jit(solution)/shard_map/ppermute | solution.py:18
  225.9 70.6 %copy-start.47 = (s32[24]{0:T(128)S(1)}, s32[24]{0:T(128)}, u32[]{:S(2)}) copy-start(s32[24]{0:T(128)} %copy-done.46) | copy-start | bytes 292
  343.9 9.5 %copy-start.10 = (bf16[4,64,1024]{2,1,0:T(8,128)(2,1)S(1)}, bf16[4,64,1024]{2,1,0:T(8,128)(2,1)}, u32[]{:S(2)}) copy-start(bf16[4,64,1024]{2,1,0:T(8,128)(2,1)} %copy-done.9) | copy-start | bytes 1572868
  347.1 62.8 %copy-start.21 = (bf16[3,64,64]{2,1,0:T(8,128)(2,1)S(1)}, bf16[3,64,64]{2,1,0:T(8,128)(2,1)}, u32[]{:S(2)}) copy-start(bf16[3,64,64]{2,1,0:T(8,128)(2,1)} %param.32) | copy-start | bytes 73732
  347.1 62.8 %copy-start.49 = (f32[64]{0:T(128)S(1)}, f32[64]{0:T(128)}, u32[]{:S(2)}) copy-start(f32[64]{0:T(128)} %get-tuple-element.21) | copy-start | bytes 772
  353.7 56.6 %collective-permute-start.5 = (bf16[256,1024]{0,1:T(8,128)(2,1)S(1)}, bf16[256,1024]{0,1:T(8,128)(2,1)S(1)}, u32[]{:S(2)}, u32[]{:S(2)}) collective-permute-start(bf16[256,1024]{0,1:T(8,128)(2,1)S(1)} %copy.198), channel_id=1, source_target_pairs={{4,0},{8,4},{12,8},{16,12},{20,16},{24,20},{28,24},{5,1},{9,5},{13... | collective-permute-start | bytes 1572872 | tf_op jit(solution)/shard_map/ppermute | solution.py:20
  355.0 56.3 %collective-permute-start.4 = (bf16[256,1024]{0,1:T(8,128)(2,1)S(1)}, bf16[256,1024]{0,1:T(8,128)(2,1)S(1)}, u32[]{:S(2)}, u32[]{:S(2)}) collective-permute-start(bf16[256,1024]{0,1:T(8,128)(2,1)S(1)} %copy.198), channel_id=1, source_target_pairs={{0,4},{4,8},{8,12},{12,16},{16,20},{20,24},{24,28},{1,5},{5,9},{9,... | collective-permute-start | bytes 1572872 | tf_op jit(solution)/shard_map/ppermute | solution.py:18
  437.6 15.1 %copy-start.30 = (f32[16,64]{1,0:T(8,128)S(1)}, f32[16,64]{1,0:T(8,128)}, u32[]{:S(2)}) copy-start(f32[16,64]{1,0:T(8,128)} %copy-done.29) | copy-start | bytes 12292
  439.2 12.3 %all-to-all-start = ((bf16[4,2,32768]{2,1,0:T(2,128)(2,1)}), bf16[4,2,32768]{2,1,0:T(2,128)(2,1)S(1)}, u32[]{:S(2)}, u32[]{:S(2)}) async-start(bf16[4,2,32768]{2,1,0:T(2,128)(2,1)} %reshape.477), calls=%async_computation.2 | async-start | bytes 1048576 | tf_op jit(solution)/shard_map/all_to_all | solution.py:175
  442.7 11.6 %copy-start.1 = (bf16[822,64]{0,1:T(8,128)(2,1)S(1)}, bf16[822,64]{0,1:T(8,128)(2,1)}, u32[]{:S(2)}) copy-start(bf16[822,64]{0,1:T(8,128)(2,1)} %param.30) | copy-start | bytes 315652
  (50 other events, 188.3 us)
Sparse Core Ops, SparseCore 0:
  49.6 62.6 reduce-scatter.3
  158.0 62.5 reduce-scatter.5
  347.9 61.0 reduce-scatter.7
where the time goes:
time: 468 us; the launch traced here: 461 us
  waiting for transfers between devices  158 us (34%)
  matrix products  107 us (23%)
  local copies, waits for them, and re-layouts  71.9 us (15%)
  blocking collectives  64.8 us (14%)
  starting transfers between devices  23.9 us (5%)
  other arithmetic  20.6 us (4%)
  between operations  15.3 us (3%)
    reduce_scatter x3, waiting for transfers between devices, body(): lax.psum_scatter(partial_value, 'ent', scatter_dimension=0, tiled=True)  150 us
    all_gather x2, blocking collectives, body(): hub_full = lax.all_gather(hub_own, 'ent', axis=0, tiled=True)  64.8 us
    dot_general x3, matrix products, body(): totals = jnp.einsum('ctk,tb->cbk', product, reg_onehot, precision=highest)  28.1 us
    dot_general x3, matrix products, body(): jnp.einsum('ctj,tjk->ctk', gathered, reg_masks, preferred_element_type=jn...  19.8 us
    gather x3, local copies, waits for them, and re-layouts, body(): gathered = jnp.take(window_blocks, reg_sources, axis=1)  17.7 us
    ppermute x3, starting transfers between devices, padded(): lax.ppermute(tail, axis, [(i, (i + 1) % count) for i in range(ends)])  16.3 us
    dot_general x3, matrix products, body(): jnp.einsum('ctk,tb->cbk', product, hout_onehot, precision=highest)  13.3 us
    dot_general x3, matrix products, body(): jnp.einsum('ctj,tjk->tkc', hin_gathered, hin_masks, preferred_element_typ...  12.6 us
  transfers between devices with their start and end apart: 10, of which 4 were waited for; matrix products, arithmetic and copies ran while one was open for 17% of the time, Pallas kernels for 0%

commit v1 on v0

--- a/solution.py
+++ b/solution.py
@@ -121,7 +121,25 @@
         product = product * tile_coefficients(reg_rel, rel_layer)[:, :, None]
         totals = jnp.einsum("ctk,tb->cbk", product, reg_onehot, precision=highest)
         if layer_at > 0:
-            hub_full = lax.all_gather(hub_own, "ent", axis=0, tiled=True)
+            length, mine, rows = (lax.axis_size("ent"), lax.axis_index("ent"), hub_own.shape[0])
+            upward = [(i_2, (i_2 + 1) % length) for i_2 in range(length)]
+            left = [(i_2, (i_2 - 1) % length) for i_2 in range(length)]
+            hub_full = jnp.zeros(
+                (*hub_own.shape[:0], length * rows, *hub_own.shape[0 + 1 :]), hub_own.dtype
+            )
+            hub_full = lax.dynamic_update_slice_in_dim(hub_full, hub_own, mine * rows, axis=0)
+            from_left = from_right = hub_own
+            halfway = length // 2
+            for step in range(1, halfway + 1):
+                from_left = lax.ppermute(from_left, "ent", upward)
+                hub_full = lax.dynamic_update_slice_in_dim(
+                    hub_full, from_left, (mine - step) % length * rows, axis=0
+                )
+                if step < length - halfway:
+                    from_right = lax.ppermute(from_right, "ent", left)
+                    hub_full = lax.dynamic_update_slice_in_dim(
+                        hub_full, from_right, (mine + step) % length * rows, axis=0
+                    )
         else:
             hub_full = jnp.zeros((hub_total, state_rows), jnp.bfloat16)
         hub_view = hub_full.reshape(hub_block_count, block_size, state_rows)

time: 468 us -> 450 us (0.962)
  blocking collectives: 64.8 us -> 0 us
  starting transfers between devices: 23.9 us -> 52.5 us
  local copies, waits for them, and re-layouts: 71.9 us -> 85.5 us
  waiting for transfers between devices: 158 us -> 163 us
    all_gather x2 -> x0, blocking collectives: 64.8 us -> none  [body(): hub_full = lax.all_gather(hub_own, 'ent', axis=0, tiled=True)]
    ppermute x0 -> x14, starting transfers between devices: none -> 28.3 us  [the longest x6 26.9 us: body(): from_right = lax.ppermute(from_right, 'ent', left)]
    dynamic_update_slice x0 -> x16, local copies, waits for them, and re-layouts: none -> 10.9 us  [the longest x8 5.43 us: body(): lax.dynamic_update_slice_in_dim(hub_full, from_left, (mine - step) % leng...]
    ppermute x0 -> x14, waiting for transfers between devices: none -> 5.02 us  [the longest x8 5 us: body(): from_left = lax.ppermute(from_left, 'ent', upward)]
  transfers between devices with their start and end apart: 10 -> 24, of which waited for: 4 -> 6; matrix products, arithmetic and copies ran while one was open for 17% -> 21% of each run, Pallas kernels for 0% -> 0%
where the time goes in v1:
time: 450 us; the launch traced here: 444 us
  waiting for transfers between devices  163 us (36%)
  matrix products  107 us (24%)
  local copies, waits for them, and re-layouts  85.5 us (19%)
  starting transfers between devices  52.5 us (12%)
  other arithmetic  20.7 us (5%)
  between operations  15.4 us (3%)
    reduce_scatter x3, waiting for transfers between devices, body(): lax.psum_scatter(partial_value, 'ent', scatter_dimension=0, tiled=True)  150 us
    dot_general x3, matrix products, body(): totals = jnp.einsum('ctk,tb->cbk', product, reg_onehot, precision=highest)  28.1 us
    ppermute x6, starting transfers between devices, body(): from_right = lax.ppermute(from_right, 'ent', left)  26.9 us
    dot_general x3, matrix products, body(): jnp.einsum('ctj,tjk->ctk', gathered, reg_masks, preferred_element_type=jn...  19.7 us
    gather x3, local copies, waits for them, and re-layouts, body(): gathered = jnp.take(window_blocks, reg_sources, axis=1)  17.6 us
    ppermute x3, starting transfers between devices, padded(): lax.ppermute(tail, axis, [(i, (i + 1) % count) for i in range(ends)])  16.3 us
    dot_general x3, matrix products, body(): jnp.einsum('ctk,tb->cbk', product, hout_onehot, precision=highest)  13.4 us
    dot_general x3, matrix products, body(): jnp.einsum('ctj,tjk->tkc', hin_gathered, hin_masks, preferred_element_typ...  12.6 us
  transfers between devices with their start and end apart: 24, of which 6 were waited for; matrix products, arithmetic and copies ran while one was open for 21% of the time, Pallas kernels for 0%

profile of v1, /device:TPU:0, one launch (start us, length us, event | category | flops | bytes accessed | tf_op | source)
XLA Modules:
  0.0 443.5 jit_solution(18056895279808356756)
XLA Ops:
  13.3 6.3 %collective-permute-start = (bf16[256,1024]{1,0:T(8,128)(2,1)}, bf16[256,1024]{1,0:T(8,128)(2,1)}, u32[]{:S(2)}, u32[]{:S(2)}) collective-permute-start(bf16[256,1024]{1,0:T(8,128)(2,1)} %fusion.90), channel_id=1, source_target_pairs={{0,4},{4,8},{8,12},{12,16},{16,20},{20,24},{24,28},{1,5},{5,9},{9,... | collective-permute-start | bytes 1572872 | tf_op jit(solution)/shard_map/ppermute | solution.py:18
  64.5 47.9 %reduce-scatter.4.cloned.1.call-done = f32[16,256]{1,0:T(8,128)} async-done(((f32[128,256]{1,0:T(8,128)}), f32[16,256]{1,0:T(8,128)}) %reduce-scatter.4.cloned.1.call-update) | async-done | bytes 16400 | tf_op jit(solution)/shard_map/reduce_scatter | solution.py:172
  117.7 5.9 %gather_fusion = bf16[80,256,128]{2,1,0:T(8,128)(2,1)} fusion(bf16[256,24,128]{2,0,1:T(8,128)(2,1)S(1)} %copy.187, s32[1024]{0:T(1024)} %pad_clamp_fusion.1), kind=kCustom, calls=%fused_computation.clone | custom fusion | bytes 10486080 | tf_op jit(solution)/shard_map/jit(_take)/gather | solution.py:117
  123.6 6.5 %bitcast_multiply_fusion.2 = f32[256,80,128]{2,0,1:T(8,128)S(1)} fusion(f32[256,80]{0,1:T(8,128)S(1)} %copy-done.19, bf16[80,256,128]{2,1,0:T(8,128)(2,1)} %gather_fusion, pred[80]{0:T(512)(128)(4,1)S(1)} %copy-done.37, s32[80,128,128]{2,1,0:T(8,128)} %param.38), kind=kOutput, calls=%fused_computation.8 | convolution fusion | flops 677642240 | bytes 21053520 | tf_op jit(solution)/shard_map/ctj,tjk->ctk/dot_general | solution.py:118
  130.2 9.4 %fusion.78 = bf16[256,8,128]{2,1,0:T(8,128)(2,1)S(1)} fusion(f32[256,8,128]{2,1,0:T(8,128)S(1)} %get-tuple-element.12, f32[8,256,128]{2,0,1:T(8,128)S(1)} %copy-done.15, f32[256,80,128]{2,0,1:T(8,128)S(1)} %bitcast_multiply_fusion.2, s32[80]{0:T(128)S(1)} %copy-done.43), kind=kOutput, calls=%fused_computation.76 | convolution fusion | flops 252445312 | bytes 13107520 | tf_op jit(solution)/shard_map/ctk,tb->cbk/dot_general | solution.py:122
  146.0 4.4 multiply_bitcast_fusion.1
  162.6 5.4 %collective-permute-start.2 = (bf16[256,1024]{0,1:T(8,128)(2,1)}, bf16[256,1024]{0,1:T(8,128)(2,1)}, u32[]{:S(2)}, u32[]{:S(2)}) collective-permute-start(bf16[256,1024]{0,1:T(8,128)(2,1)} %copy.193), channel_id=1, source_target_pairs={{0,4},{4,8},{8,12},{12,16},{16,20},{20,24},{24,28},{1,5},{5,9},{9,... | collective-permute-start | bytes 1572872 | tf_op jit(solution)/shard_map/ppermute | solution.py:18
  167.9 52.5 %reduce-scatter.6.cloned.1.call-done = f32[16,256]{1,0:T(8,128)} async-done(((f32[128,256]{1,0:T(8,128)}), f32[16,256]{1,0:T(8,128)}) %reduce-scatter.6.cloned.1.call-update) | async-done | bytes 16400 | tf_op jit(solution)/shard_map/reduce_scatter | solution.py:172
  235.2 4.7 %collective-permute-start.14 = (bf16[16,256]{1,0:T(8,128)(2,1)}, bf16[16,256]{1,0:T(8,128)(2,1)S(1)}, u32[]{:S(2)}, u32[]{:S(2)}) collective-permute-start(bf16[16,256]{1,0:T(8,128)(2,1)} %reshape.452), channel_id=1, source_target_pairs={{0,28},{4,0},{8,4},{12,8},{16,12},{20,16},{24,20},{28,24},{1,29},{... | collective-permute-start | bytes 24584 | tf_op jit(solution)/shard_map/ppermute | solution.py:139
  242.5 4.7 %collective-permute-start.7 = (bf16[16,256]{1,0:T(8,128)(2,1)}, bf16[16,256]{1,0:T(8,128)(2,1)S(1)}, u32[]{:S(2)}, u32[]{:S(2)}) collective-permute-start(bf16[16,256]{1,0:T(8,128)(2,1)} %collective-permute-done.5), channel_id=1, source_target_pairs={{0,28},{4,0},{8,4},{12,8},{16,12},{20,16},{24,20},{28,24},{1,29},{... | collective-permute-start | bytes 24584 | tf_op jit(solution)/shard_map/ppermute | solution.py:139
  248.4 4.7 %collective-permute-start.16 = (bf16[16,256]{1,0:T(8,128)(2,1)S(1)}, bf16[16,256]{1,0:T(8,128)(2,1)S(1)}, u32[]{:S(2)}, u32[]{:S(2)}) collective-permute-start(bf16[16,256]{1,0:T(8,128)(2,1)S(1)} %collective-permute-done.14), channel_id=1, source_target_pairs={{0,28},{4,0},{8,4},{12,8},{16,12},{20,16},{24,20},{28,24},{1,29},{... | collective-permute-start | bytes 24584 | tf_op jit(solution)/shard_map/ppermute | solution.py:139
  254.3 4.7 %collective-permute-start.9 = (bf16[16,256]{1,0:T(8,128)(2,1)S(1)}, bf16[16,256]{1,0:T(8,128)(2,1)S(1)}, u32[]{:S(2)}, u32[]{:S(2)}) collective-permute-start(bf16[16,256]{1,0:T(8,128)(2,1)S(1)} %collective-permute-done.7), channel_id=1, source_target_pairs={{0,28},{4,0},{8,4},{12,8},{16,12},{20,16},{24,20},{28,24},{1,29},{... | collective-permute-start | bytes 24584 | tf_op jit(solution)/shard_map/ppermute | solution.py:139
  260.2 4.7 %collective-permute-start.18 = (bf16[16,256]{1,0:T(8,128)(2,1)S(1)}, bf16[16,256]{1,0:T(8,128)(2,1)S(1)}, u32[]{:S(2)}, u32[]{:S(2)}) collective-permute-start(bf16[16,256]{1,0:T(8,128)(2,1)S(1)} %collective-permute-done.16), channel_id=1, source_target_pairs={{0,28},{4,0},{8,4},{12,8},{16,12},{20,16},{24,20},{28,24},{1,29},{... | collective-permute-start | bytes 24584 | tf_op jit(solution)/shard_map/ppermute | solution.py:139
  267.8 4.6 %collective-permute-done.10 = bf16[16,256]{1,0:T(8,128)(2,1)S(1)} collective-permute-done((bf16[16,256]{1,0:T(8,128)(2,1)S(1)}, bf16[16,256]{1,0:T(8,128)(2,1)S(1)}, u32[]{:S(2)}, u32[]{:S(2)}) %collective-permute-start.10) | collective-permute-done | bytes 8224 | tf_op jit(solution)/shard_map/ppermute | solution.py:134
  290.2 5.9 %gather_fusion.1 = bf16[80,256,128]{2,1,0:T(8,128)(2,1)} fusion(bf16[256,24,128]{2,0,1:T(8,128)(2,1)S(1)} %pad_maximum_fusion.1, s32[1024]{0:T(1024)} %pad_clamp_fusion.1), kind=kCustom, calls=%fused_computation.2.clone | custom fusion | bytes 10486080 | tf_op jit(solution)/shard_map/jit(_take)/gather | solution.py:117
  296.2 6.5 %bitcast_multiply_fusion.1 = f32[256,80,128]{2,0,1:T(8,128)S(1)} fusion(f32[256,80]{0,1:T(8,128)S(1)} %copy-done.18, bf16[80,256,128]{2,1,0:T(8,128)(2,1)} %gather_fusion.1, pred[80]{0:T(512)(128)(4,1)S(1)} %copy-done.38, s32[80,128,128]{2,1,0:T(8,128)} %param.38), kind=kOutput, calls=%fused_computation.7 | convolution fusion | flops 677642240 | bytes 21053520 | tf_op jit(solution)/shard_map/ctj,tjk->ctk/dot_general | solution.py:118
  302.7 9.4 %fusion.81 = bf16[256,8,128]{2,1,0:T(8,128)(2,1)S(1)} fusion(f32[256,8,128]{2,1,0:T(8,128)S(1)} %get-tuple-element.12, f32[8,256,128]{2,0,1:T(8,128)S(1)} %copy-done.17, f32[256,80,128]{2,0,1:T(8,128)S(1)} %bitcast_multiply_fusion.1, s32[80]{0:T(128)S(1)} %copy-done.44), kind=kOutput, calls=%fused_computation.77 | convolution fusion | flops 252445312 | bytes 13107520 | tf_op jit(solution)/shard_map/ctk,tb->cbk/dot_general | solution.py:122
  329.8 5.7 %fusion.24 = f32[8,256,128]{2,0,1:T(8,128)} fusion(f32[256,24,128]{2,0,1:T(8,128)} %bitcast_multiply_fusion.3, s32[24]{0:T(128)S(1)} %copy-done.48), kind=kOutput, calls=%fused_computation.30 | convolution fusion | flops 75497664 | bytes 4194400 | tf_op jit(solution)/shard_map/ctk,tb->cbk/dot_general | solution.py:151
  337.0 4.6 %collective-permute-start.11 = (bf16[256,1024]{0,1:T(8,128)(2,1)S(1)}, bf16[256,1024]{0,1:T(8,128)(2,1)S(1)}, u32[]{:S(2)}, u32[]{:S(2)}) collective-permute-start(bf16[256,1024]{0,1:T(8,128)(2,1)S(1)} %copy.208), channel_id=1, source_target_pairs={{0,4},{4,8},{8,12},{12,16},{16,20},{20,24},{24,28},{1,5},{5,9},{9,... | collective-permute-start | bytes 1572872 | tf_op jit(solution)/shard_map/ppermute | solution.py:18
  341.6 49.7 %reduce-scatter.8.cloned.1.call-done = f32[16,256]{1,0:T(8,128)} async-done(((f32[128,256]{1,0:T(8,128)}), f32[16,256]{1,0:T(8,128)}) %reduce-scatter.8.cloned.1.call-update) | async-done | bytes 16400 | tf_op jit(solution)/shard_map/reduce_scatter | solution.py:172
  396.0 5.8 %gather_fusion.3 = bf16[80,256,128]{2,1,0:T(8,128)(2,1)} fusion(bf16[256,24,128]{2,0,1:T(8,128)(2,1)S(1)} %pad_maximum_fusion.2, s32[1024]{0:T(1024)} %pad_clamp_fusion.1), kind=kCustom, calls=%fused_computation.3.clone | custom fusion | bytes 10486080 | tf_op jit(solution)/shard_map/jit(_take)/gather | solution.py:117
  401.7 6.6 %bitcast_multiply_fusion = f32[256,80,128]{2,0,1:T(8,128)S(1)} fusion(f32[256,80]{0,1:T(8,128)S(1)} %copy.213, bf16[80,256,128]{2,1,0:T(8,128)(2,1)} %gather_fusion.3, pred[80]{0:T(512)(128)(4,1)S(1)} %copy-done.38, s32[80,128,128]{2,1,0:T(8,128)} %param.38), kind=kOutput, calls=%fused_computation.6 | convolution fusion | flops 677642240 | bytes 21053520 | tf_op jit(solution)/shard_map/ctj,tjk->ctk/dot_general | solution.py:118
  408.4 9.4 %fusion.84 = bf16[256,8,128]{2,1,0:T(8,128)(2,1)S(1)} fusion(f32[256,8,128]{2,1,0:T(8,128)S(1)} %get-tuple-element.12, f32[8,256,128]{2,0,1:T(8,128)S(1)} %copy-done.16, f32[256,80,128]{2,0,1:T(8,128)S(1)} %bitcast_multiply_fusion, s32[80]{0:T(128)S(1)} %copy-done.45), kind=kOutput, calls=%fused_computation.78 | convolution fusion | flops 252445312 | bytes 13107520 | tf_op jit(solution)/shard_map/ctk,tb->cbk/dot_general | solution.py:122
  426.1 7.6 %all-to-all-done = bf16[4,2,32768]{2,1,0:T(2,128)(2,1)S(1)} async-done(((bf16[4,2,32768]{2,1,0:T(2,128)(2,1)}), bf16[4,2,32768]{2,1,0:T(2,128)(2,1)S(1)}, u32[]{:S(2)}, u32[]{:S(2)}) %all-to-all-start) | async-done | bytes 524320 | tf_op jit(solution)/shard_map/all_to_all | solution.py:193
  (324 shorter events, 150.5 us)
Async XLA Ops:
  7.2 105.3 %reduce-scatter.4.cloned.1.call-start = ((), (), s32[]{:S(2)}) async-start(), calls=%async_computation.4 | async-start | bytes 147456 | tf_op jit(solution)/shard_map/reduce_scatter | solution.py:172
  12.1 102.7 %collective-permute-start.1 = (bf16[256,1024]{1,0:T(8,128)(2,1)}, bf16[256,1024]{1,0:T(8,128)(2,1)}, u32[]{:S(2)}, u32[]{:S(2)}) collective-permute-start(bf16[256,1024]{1,0:T(8,128)(2,1)} %fusion.90), channel_id=1, source_target_pairs={{4,0},{8,4},{12,8},{16,12},{20,16},{24,20},{28,24},{5,1},{9,5},{13... | collective-permute-start | bytes 1572872 | tf_op jit(solution)/shard_map/ppermute | solution.py:20
  13.3 102.5 %collective-permute-start = (bf16[256,1024]{1,0:T(8,128)(2,1)}, bf16[256,1024]{1,0:T(8,128)(2,1)}, u32[]{:S(2)}, u32[]{:S(2)}) collective-permute-start(bf16[256,1024]{1,0:T(8,128)(2,1)} %fusion.90), channel_id=1, source_target_pairs={{0,4},{4,8},{8,12},{12,16},{16,20},{20,24},{24,28},{1,5},{5,9},{9,... | collective-permute-start | bytes 1572872 | tf_op jit(solution)/shard_map/ppermute | solution.py:18
  49.5 171.0 %reduce-scatter.6.cloned.1.call-start = ((), (), s32[]{:S(2)}) async-start(), calls=%async_computation.5 | async-start | bytes 147456 | tf_op jit(solution)/shard_map/reduce_scatter | solution.py:172
  157.8 233.5 %reduce-scatter.8.cloned.1.call-start = ((), (), s32[]{:S(2)}) async-start(), calls=%async_computation.6 | async-start | bytes 147456 | tf_op jit(solution)/shard_map/reduce_scatter | solution.py:172
  161.3 123.4 %collective-permute-start.3 = (bf16[256,1024]{0,1:T(8,128)(2,1)}, bf16[256,1024]{0,1:T(8,128)(2,1)}, u32[]{:S(2)}, u32[]{:S(2)}) collective-permute-start(bf16[256,1024]{0,1:T(8,128)(2,1)} %copy.193), channel_id=1, source_target_pairs={{4,0},{8,4},{12,8},{16,12},{20,16},{24,20},{28,24},{5,1},{9,5},{13... | collective-permute-start | bytes 1572872 | tf_op jit(solution)/shard_map/ppermute | solution.py:20
  162.6 124.2 %collective-permute-start.2 = (bf16[256,1024]{0,1:T(8,128)(2,1)}, bf16[256,1024]{0,1:T(8,128)(2,1)}, u32[]{:S(2)}, u32[]{:S(2)}) collective-permute-start(bf16[256,1024]{0,1:T(8,128)(2,1)} %copy.193), channel_id=1, source_target_pairs={{0,4},{4,8},{8,12},{12,16},{16,20},{20,24},{24,28},{1,5},{5,9},{9,... | collective-permute-start | bytes 1572872 | tf_op jit(solution)/shard_map/ppermute | solution.py:18
  226.5 8.7 %collective-permute-start.4 = (bf16[16,256]{1,0:T(8,128)(2,1)}, bf16[16,256]{1,0:T(8,128)(2,1)}, u32[]{:S(2)}, u32[]{:S(2)}) collective-permute-start(bf16[16,256]{1,0:T(8,128)(2,1)} %reshape.441), channel_id=1, source_target_pairs={{0,4},{4,8},{8,12},{12,16},{16,20},{20,24},{24,28},{28,0},{1,5},{5... | collective-permute-start | bytes 24584 | tf_op jit(solution)/shard_map/ppermute | solution.py:134
  227.9 13.2 %collective-permute-start.5 = (bf16[16,256]{1,0:T(8,128)(2,1)}, bf16[16,256]{1,0:T(8,128)(2,1)}, u32[]{:S(2)}, u32[]{:S(2)}) collective-permute-start(bf16[16,256]{1,0:T(8,128)(2,1)} %reshape.441), channel_id=1, source_target_pairs={{0,28},{4,0},{8,4},{12,8},{16,12},{20,16},{24,20},{28,24},{1,29},{... | collective-permute-start | bytes 24584 | tf_op jit(solution)/shard_map/ppermute | solution.py:139
  232.7 9.8 %collective-permute-start.13 = (bf16[16,256]{1,0:T(8,128)(2,1)}, bf16[16,256]{1,0:T(8,128)(2,1)S(1)}, u32[]{:S(2)}, u32[]{:S(2)}) collective-permute-start(bf16[16,256]{1,0:T(8,128)(2,1)} %reshape.452), channel_id=1, source_target_pairs={{0,4},{4,8},{8,12},{12,16},{16,20},{20,24},{24,28},{28,0},{1,5},{5... | collective-permute-start | bytes 24584 | tf_op jit(solution)/shard_map/ppermute | solution.py:134
  235.2 12.6 %collective-permute-start.14 = (bf16[16,256]{1,0:T(8,128)(2,1)}, bf16[16,256]{1,0:T(8,128)(2,1)S(1)}, u32[]{:S(2)}, u32[]{:S(2)}) collective-permute-start(bf16[16,256]{1,0:T(8,128)(2,1)} %reshape.452), channel_id=1, source_target_pairs={{0,28},{4,0},{8,4},{12,8},{16,12},{20,16},{24,20},{28,24},{1,29},{... | collective-permute-start | bytes 24584 | tf_op jit(solution)/shard_map/ppermute | solution.py:139
  241.2 7.2 %collective-permute-start.6 = (bf16[16,256]{1,0:T(8,128)(2,1)}, bf16[16,256]{1,0:T(8,128)(2,1)S(1)}, u32[]{:S(2)}, u32[]{:S(2)}) collective-permute-start(bf16[16,256]{1,0:T(8,128)(2,1)} %collective-permute-done.4), channel_id=1, source_target_pairs={{0,4},{4,8},{8,12},{12,16},{16,20},{20,24},{24,28},{28,0},{1,5},{5... | collective-permute-start | bytes 24584 | tf_op jit(solution)/shard_map/ppermute | solution.py:134
  242.5 11.2 %collective-permute-start.7 = (bf16[16,256]{1,0:T(8,128)(2,1)}, bf16[16,256]{1,0:T(8,128)(2,1)S(1)}, u32[]{:S(2)}, u32[]{:S(2)}) collective-permute-start(bf16[16,256]{1,0:T(8,128)(2,1)} %collective-permute-done.5), channel_id=1, source_target_pairs={{0,28},{4,0},{8,4},{12,8},{16,12},{20,16},{24,20},{28,24},{1,29},{... | collective-permute-start | bytes 24584 | tf_op jit(solution)/shard_map/ppermute | solution.py:139
  247.8 6.5 %collective-permute-start.15 = (bf16[16,256]{1,0:T(8,128)(2,1)S(1)}, bf16[16,256]{1,0:T(8,128)(2,1)S(1)}, u32[]{:S(2)}, u32[]{:S(2)}) collective-permute-start(bf16[16,256]{1,0:T(8,128)(2,1)S(1)} %collective-permute-done.13), channel_id=1, source_target_pairs={{0,4},{4,8},{8,12},{12,16},{16,20},{20,24},{24,28},{28,0},{1,5},{5... | collective-permute-start | bytes 24584 | tf_op jit(solution)/shard_map/ppermute | solution.py:134
  248.4 11.3 %collective-permute-start.16 = (bf16[16,256]{1,0:T(8,128)(2,1)S(1)}, bf16[16,256]{1,0:T(8,128)(2,1)S(1)}, u32[]{:S(2)}, u32[]{:S(2)}) collective-permute-start(bf16[16,256]{1,0:T(8,128)(2,1)S(1)} %collective-permute-done.14), channel_id=1, source_target_pairs={{0,28},{4,0},{8,4},{12,8},{16,12},{20,16},{24,20},{28,24},{1,29},{... | collective-permute-start | bytes 24584 | tf_op jit(solution)/shard_map/ppermute | solution.py:139
  253.7 6.5 %collective-permute-start.8 = (bf16[16,256]{1,0:T(8,128)(2,1)S(1)}, bf16[16,256]{1,0:T(8,128)(2,1)S(1)}, u32[]{:S(2)}, u32[]{:S(2)}) collective-permute-start(bf16[16,256]{1,0:T(8,128)(2,1)S(1)} %collective-permute-done.6), channel_id=1, source_target_pairs={{0,4},{4,8},{8,12},{12,16},{16,20},{20,24},{24,28},{28,0},{1,5},{5... | collective-permute-start | bytes 24584 | tf_op jit(solution)/shard_map/ppermute | solution.py:134
  254.3 12.3 %collective-permute-start.9 = (bf16[16,256]{1,0:T(8,128)(2,1)S(1)}, bf16[16,256]{1,0:T(8,128)(2,1)S(1)}, u32[]{:S(2)}, u32[]{:S(2)}) collective-permute-start(bf16[16,256]{1,0:T(8,128)(2,1)S(1)} %collective-permute-done.7), channel_id=1, source_target_pairs={{0,28},{4,0},{8,4},{12,8},{16,12},{20,16},{24,20},{28,24},{1,29},{... | collective-permute-start | bytes 24584 | tf_op jit(solution)/shard_map/ppermute | solution.py:139
  259.6 6.3 %collective-permute-start.17 = (bf16[16,256]{1,0:T(8,128)(2,1)S(1)}, bf16[16,256]{1,0:T(8,128)(2,1)S(1)}, u32[]{:S(2)}, u32[]{:S(2)}) collective-permute-start(bf16[16,256]{1,0:T(8,128)(2,1)S(1)} %collective-permute-done.15), channel_id=1, source_target_pairs={{0,4},{4,8},{8,12},{12,16},{16,20},{20,24},{24,28},{28,0},{1,5},{5... | collective-permute-start | bytes 24584 | tf_op jit(solution)/shard_map/ppermute | solution.py:134
  260.2 6.9 %collective-permute-start.18 = (bf16[16,256]{1,0:T(8,128)(2,1)S(1)}, bf16[16,256]{1,0:T(8,128)(2,1)S(1)}, u32[]{:S(2)}, u32[]{:S(2)}) collective-permute-start(bf16[16,256]{1,0:T(8,128)(2,1)S(1)} %collective-permute-done.16), channel_id=1, source_target_pairs={{0,28},{4,0},{8,4},{12,8},{16,12},{20,16},{24,20},{28,24},{1,29},{... | collective-permute-start | bytes 24584 | tf_op jit(solution)/shard_map/ppermute | solution.py:139
  266.0 6.3 %collective-permute-start.10 = (bf16[16,256]{1,0:T(8,128)(2,1)S(1)}, bf16[16,256]{1,0:T(8,128)(2,1)S(1)}, u32[]{:S(2)}, u32[]{:S(2)}) collective-permute-start(bf16[16,256]{1,0:T(8,128)(2,1)S(1)} %collective-permute-done.8), channel_id=1, source_target_pairs={{0,4},{4,8},{8,12},{12,16},{16,20},{20,24},{24,28},{28,0},{1,5},{5... | collective-permute-start | bytes 24584 | tf_op jit(solution)/shard_map/ppermute | solution.py:134
  266.6 7.9 %collective-permute-start.19 = (bf16[16,256]{1,0:T(8,128)(2,1)S(1)}, bf16[16,256]{1,0:T(8,128)(2,1)S(1)}, u32[]{:S(2)}, u32[]{:S(2)}) collective-permute-start(bf16[16,256]{1,0:T(8,128)(2,1)S(1)} %collective-permute-done.17), channel_id=1, source_target_pairs={{0,4},{4,8},{8,12},{12,16},{16,20},{20,24},{24,28},{28,0},{1,5},{5... | collective-permute-start | bytes 24584 | tf_op jit(solution)/shard_map/ppermute | solution.py:134
  335.7 56.8 %collective-permute-start.12 = (bf16[256,1024]{0,1:T(8,128)(2,1)S(1)}, bf16[256,1024]{0,1:T(8,128)(2,1)S(1)}, u32[]{:S(2)}, u32[]{:S(2)}) collective-permute-start(bf16[256,1024]{0,1:T(8,128)(2,1)S(1)} %copy.208), channel_id=1, source_target_pairs={{4,0},{8,4},{12,8},{16,12},{20,16},{24,20},{28,24},{5,1},{9,5},{13... | collective-permute-start | bytes 1572872 | tf_op jit(solution)/shard_map/ppermute | solution.py:20
  337.0 56.6 %collective-permute-start.11 = (bf16[256,1024]{0,1:T(8,128)(2,1)S(1)}, bf16[256,1024]{0,1:T(8,128)(2,1)S(1)}, u32[]{:S(2)}, u32[]{:S(2)}) collective-permute-start(bf16[256,1024]{0,1:T(8,128)(2,1)S(1)} %copy.208), channel_id=1, source_target_pairs={{0,4},{4,8},{8,12},{12,16},{16,20},{20,24},{24,28},{1,5},{5,9},{9,... | collective-permute-start | bytes 1572872 | tf_op jit(solution)/shard_map/ppermute | solution.py:18
  421.5 12.3 %all-to-all-start = ((bf16[4,2,32768]{2,1,0:T(2,128)(2,1)}), bf16[4,2,32768]{2,1,0:T(2,128)(2,1)S(1)}, u32[]{:S(2)}, u32[]{:S(2)}) async-start(bf16[4,2,32768]{2,1,0:T(2,128)(2,1)} %reshape.553), calls=%async_computation.2 | async-start | bytes 1048576 | tf_op jit(solution)/shard_map/all_to_all | solution.py:193
  (64 other events, 727.3 us)
Sparse Core Ops, SparseCore 0:
  49.6 62.7 reduce-scatter.3
  157.9 62.5 reduce-scatter.5
  329.9 61.3 reduce-scatter.7
